TPU v7x, 512 devices: a whole 4x4x16 slice. The times are simulated.
512 devices in a mesh: row: 8 (over x, core), col: 16 (over z), layer: 4 (over y).
Axes of the slice: x: 4, y: 4, z: 16, core: 2. Of those that a mesh axis runs over, the one named last changes fastest.
Arguments:
- occurrences: bfloat16 [8192, 10240], P(('row', 'col', 'layer')), may hold values from -6 to 6
- idf_weight: float32 [8192], P(('row', 'col', 'layer')), may hold values from 0.25 to 2
- pattern: int32 [64, 80], replicated, may hold values 0 or 1
Outputs:
- margin: bfloat16 [10240, 10240], P('row', 'col')
All inputs are finite; a program needn't handle non-finite values.
Results may differ from a plain program's by a relative error of at most 0.0058.
Values may be sent and summed in bfloat16 or wider, within the bound.
No kernel may reach another device: no remote copies, remote signals or barrier semaphores. Data moves between devices by JAX's collectives and lax.ppermute only.
A program may use at most 64 MiB of HBM per device.

v0:
```python
import math
import jax
import jax.numpy as jnp
from jax import lax
from jax.sharding import PartitionSpec as P


def finish(partial_rows, row_start, col_start, factor):
    row_ids = row_start + lax.broadcasted_iota(jnp.int32, partial_rows.shape, 0)
    col_ids = col_start + lax.broadcasted_iota(jnp.int32, partial_rows.shape, 1)
    result = jnp.where(row_ids == col_ids, jnp.float32(0.0), partial_rows * factor)
    return result.astype(jnp.bfloat16)


def body(occurrences, idf_weight, pattern):
    owned, reads = occurrences.shape
    n_rows = lax.axis_size("row")
    n_cols = lax.axis_size("col")
    n_layers = lax.axis_size("layer")
    factor = 1.0 / math.sqrt(owned * n_rows * n_cols * n_layers)
    owner = lax.axis_index(("row", "col", "layer"))
    block_row = owner * owned // 128
    flags = lax.dynamic_slice_in_dim(pattern, block_row, 1, 0)[0]
    read_mask = jnp.repeat(flags.astype(jnp.float32), 128)
    weighted = (occurrences.astype(jnp.float32) * idf_weight[:, None] * read_mask[None, :]).astype(
        jnp.bfloat16
    )
    piece_len = reads // (n_rows * n_cols)
    reordered = (
        weighted.reshape(owned, n_cols, n_rows, piece_len)
        .transpose(0, 2, 1, 3)
        .reshape(owned, reads)
    )
    row_part, col_part = (
        lax.all_to_all(weighted, ("row", "col"), split_axis=1, concat_axis=0, tiled=True),
        lax.all_to_all(reordered, ("row", "col"), split_axis=1, concat_axis=0, tiled=True),
    )
    column_reads = lax.all_gather(col_part, "row", axis=1, tiled=True)
    partial_tile = lax.dot_general(
        lax.all_gather(row_part, "col", axis=1, tiled=True),
        column_reads,
        (((0,), (0,)), ((), ())),
        preferred_element_type=jnp.float32,
    )
    row_count = partial_tile.shape[0]
    row_start = lax.axis_index("row") * row_count
    col_start = lax.axis_index("col") * partial_tile.shape[1]
    total = lax.psum(partial_tile, "layer")
    return finish(total, row_start, col_start, factor)


def solution(mesh):
    placed = (P(("row", "col", "layer"), None), P(("row", "col", "layer")), P())
    return jax.shard_map(
        body, mesh=mesh, in_specs=placed, out_specs=P("row", "col"), check_vma=False
    )
```

profile of v0, /device:TPU:1, one launch (start us, length us, event | category | flops | bytes accessed | tf_op | source)
XLA Modules:
  0.0 287.5 jit_solution(10885676402827663510)
XLA Ops:
  6.5 0.0 all-gather.5.cloned.1.call-start
  6.5 0.7 convert_bitcast_fusion
  7.2 0.1 broadcast_bitcast_fusion
  7.3 1.1 multiply_convert_fusion
  8.4 0.6 reshape.14
  9.1 0.1 copy.9
  9.2 0.3 copy.10
  9.6 52.5 %all_to_all.38 = bf16[16,128,80]{2,0,1:T(8,128)(2,1)S(1)} all-to-all(bf16[16,128,80]{2,0,1:T(8,128)(2,1)S(1)} %copy.10), channel_id=1, replica_groups=mesh['row'=8,'col'=16,'layer'=4] {'row','col'}, dimensions={1} | all-to-all | bytes 655360 | tf_op jit(solution)/shard_map/all_to_all | solution.py:36
  62.0 0.9 copy.11
  63.0 0.0 all-gather.5.cloned.1.call-update
  63.0 0.0 all-gather.3.cloned.1.call-start
  63.0 0.6 all_to_all.28
  63.7 0.3 copy.7
  64.0 39.7 %all_to_all.39 = bf16[16,128,80]{2,0,1:T(8,128)(2,1)S(1)} all-to-all(bf16[16,128,80]{2,0,1:T(8,128)(2,1)S(1)} %copy.7), channel_id=1, replica_groups=mesh['row'=8,'col'=16,'layer'=4] {'row','col'}, dimensions={1} | all-to-all | bytes 655360 | tf_op jit(solution)/shard_map/all_to_all | solution.py:35
  103.8 0.9 copy.8
  104.7 0.0 all-gather.3.cloned.1.call-update
  104.7 0.0 all-reduce.2.cloned.1.call-start
  104.8 0.0 all-gather.5.cloned.1.call-done
  104.8 67.3 %all-gather.3.cloned.1.call-done = bf16[2048,1280]{0,1:T(8,128)(2,1)} async-done(((bf16[2048,80]{0,1:T(8,128)(2,1)}), bf16[2048,1280]{0,1:T(8,128)(2,1)}) %all-gather.3.cloned.1.call-update) | async-done | bytes 5242896 | tf_op jit(solution)/shard_map/all_gather | solution.py:40
  172.1 9.3 %fusion = f32[1280,640]{1,0:T(8,128)} fusion(bf16[2048,1280]{0,1:T(8,128)(2,1)} %all-gather.3.cloned.1.call-done, bf16[2048,640]{0,1:T(8,128)(2,1)} %all-gather.5.cloned.1.call-done), kind=kOutput, calls=%fused_computation.6 | convolution fusion | flops 3355443200 | bytes 11141120 | tf_op jit(solution)/shard_map/dot_general | solution.py:39
  181.3 0.0 all-reduce.2.cloned.1.call-update
  181.4 96.0 %all-reduce.2.cloned.1.call-done = f32[1280,640]{1,0:T(8,128)} async-done(((f32[1280,640]{1,0:T(8,128)}), f32[1280,640]{1,0:T(8,128)}) %all-reduce.2.cloned.1.call-update) | async-done | bytes 3276816 | tf_op jit(solution)/shard_map/psum | solution.py:48
  277.4 3.5 %select_convert_fusion = bf16[1280,640]{1,0:T(8,128)(2,1)} fusion(f32[1280,640]{1,0:T(8,128)} %all-reduce.2.cloned.1.call-done, s32[640]{0:T(1024)S(1)} %iota_add_fusion.1, s32[1280]{0:T(1024)S(1)} %iota_add_fusion), kind=kLoop, calls=%fused_computation | loop fusion | flops 3276800 | bytes 4922880 | tf_op jit(solution)/shard_map/convert_element_type | solution.py:12
  (2 shorter events, 0.0 us)
Async XLA Ops:
  6.5 98.3 %all-gather.5.cloned.1.call-start = ((), (), s32[]{:S(2)}) async-start(), calls=%async_computation.3 | async-start | bytes 2949120 | tf_op jit(solution)/shard_map/all_gather | solution.py:38
  63.0 109.1 %all-gather.3.cloned.1.call-start = ((), (), s32[]{:S(2)}) async-start(), calls=%async_computation.2 | async-start | bytes 5570560 | tf_op jit(solution)/shard_map/all_gather | solution.py:40
  104.7 172.7 %all-reduce.2.cloned.1.call-start = ((), (), s32[]{:S(2)}) async-start(), calls=%async_computation.4 | async-start | bytes 6553600 | tf_op jit(solution)/shard_map/psum | solution.py:48
Sparse Core Ops, SparseCore 0:
  63.1 29.0 all-gather.4
  104.9 67.1 all-gather.2
  181.5 95.8 all-reduce.1
where the time goes:
time: 288 us; the launch traced here: 287 us
  waiting for transfers between devices  163 us (57%)
  blocking collectives  92.2 us (32%)
  between operations  13.2 us (5%)
  matrix products  9.28 us (3%)
  other arithmetic  5.36 us (2%)
  local copies, waits for them, and re-layouts  4.02 us (1%)
    psum x1, waiting for transfers between devices, body(): total = lax.psum(partial_tile, 'layer')  96 us
    all_gather x1, waiting for transfers between devices, body(): lax.all_gather(row_part, 'col', axis=1, tiled=True)  67.3 us
    all_to_all x1, blocking collectives, body(): lax.all_to_all(reordered, ('row', 'col'), split_axis=1, concat_axis=0, ti...  52.5 us
    all_to_all x1, blocking collectives, body(): lax.all_to_all(weighted, ('row', 'col'), split_axis=1, concat_axis=0, til...  39.7 us
    dot_general x1, matrix products, body(): lax.dot_general(lax.all_gather(row_part, 'col', axis=1, tiled=True), colu...  9.28 us
  transfers between devices with their start and end apart: 3, of which 2 were waited for; matrix products, arithmetic and copies ran while one was open for 0% of the time, Pallas kernels for 0%

commit v1 on v0

--- a/solution.py
+++ b/solution.py
@@ -1,8 +1,19 @@
+import functools
 import math
 import jax
 import jax.numpy as jnp
 from jax import lax
 from jax.sharding import PartitionSpec as P
+
+
+def order_values(xs, named_axis):
+    z_new = jnp.stack([xs for _ in range(lax.axis_size(named_axis))])
+    g_now = lax.all_to_all(z_new, axis_name=named_axis, split_axis=0, concat_axis=0)
+    parts_out = jnp.concatenate(g_now, axis=1)
+    return parts_out
+
+
+play_heaps_over_axis = functools.partial(order_values, named_axis="col")
 
 
 def finish(partial_rows, row_start, col_start, factor):
@@ -37,7 +48,7 @@
     )
     column_reads = lax.all_gather(col_part, "row", axis=1, tiled=True)
     partial_tile = lax.dot_general(
-        lax.all_gather(row_part, "col", axis=1, tiled=True),
+        play_heaps_over_axis(row_part),
         column_reads,
         (((0,), (0,)), ((), ())),
         preferred_element_type=jnp.float32,

time: 288 us -> 451 us (1.57)
  waiting for transfers between devices: 163 us -> 381 us
  blocking collectives: 92.2 us -> 0 us
  starting transfers between devices: 0.09 us -> 33.4 us
    all_to_all x0 -> x3, waiting for transfers between devices: none -> 253 us  [the longest x1 190 us: order_values(): lax.all_to_all(z_new, axis_name=named_axis, split_axis=0, concat_axis=0)]
    all_to_all x2 -> x0, blocking collectives: 92.2 us -> none  [the longest x1 52.5 us: body(): lax.all_to_all(reordered, ('row', 'col'), split_axis=1, concat_axis=0, ti...]
    all_gather x1 -> x0, waiting for transfers between devices: 67.3 us -> none  [body(): lax.all_gather(row_part, 'col', axis=1, tiled=True)]
    all_gather x1, waiting for transfers between devices: 0.02 us -> 35.4 us  [body(): column_reads = lax.all_gather(col_part, 'row', axis=1, tiled=True)]
    all_to_all x0 -> x3, starting transfers between devices: none -> 33.3 us  [the longest x1 20.4 us: body(): lax.all_to_all(weighted, ('row', 'col'), split_axis=1, concat_axis=0, til...]
  transfers between devices with their start and end apart: 3 -> 5, of which waited for: 2 -> 5; matrix products, arithmetic and copies ran while one was open for 0% -> 1% of each run, Pallas kernels for 0% -> 0%
where the time goes in v1:
time: 451 us; the launch traced here: 450 us
  waiting for transfers between devices  381 us (84%)
  starting transfers between devices  33.4 us (7%)
  between operations  13.5 us (3%)
  matrix products  9.29 us (2%)
  local copies, waits for them, and re-layouts  7.87 us (2%)
  other arithmetic  5.36 us (1%)
    all_to_all x1, waiting for transfers between devices, order_values(): lax.all_to_all(z_new, axis_name=named_axis, split_axis=0, concat_axis=0)  190 us
    psum x1, waiting for transfers between devices, body(): total = lax.psum(partial_tile, 'layer')  92.6 us
    all_gather x1, waiting for transfers between devices, body(): column_reads = lax.all_gather(col_part, 'row', axis=1, tiled=True)  35.4 us
    all_to_all x1, waiting for transfers between devices, body(): lax.all_to_all(reordered, ('row', 'col'), split_axis=1, concat_axis=0, ti...  32.1 us
    all_to_all x1, waiting for transfers between devices, body(): lax.all_to_all(weighted, ('row', 'col'), split_axis=1, concat_axis=0, til...  30.4 us
    all_to_all x1, starting transfers between devices, body(): lax.all_to_all(weighted, ('row', 'col'), split_axis=1, concat_axis=0, til...  20.4 us
    dot_general x1, matrix products, body(): lax.dot_general(play_heaps_over_axis(row_part), column_reads, (((0,), (0,...  9.29 us
  transfers between devices with their start and end apart: 5, of which 5 were waited for; matrix products, arithmetic and copies ran while one was open for 1% of the time, Pallas kernels for 0%

profile of v1, /device:TPU:1, one launch (start us, length us, event | category | flops | bytes accessed | tf_op | source)
XLA Modules:
  0.0 450.2 jit_solution(14905706455424459621)
XLA Ops:
  6.5 0.7 convert_bitcast_fusion
  7.2 0.1 broadcast_bitcast_fusion
  7.3 1.1 multiply_convert_fusion
  8.4 0.6 all_to_all.29
  9.1 1.1 copy.8
  10.2 20.4 %all-to-all-start = ((bf16[16,128,80]{2,0,1:T(8,128)(2,1)}), bf16[16,128,80]{2,0,1:T(8,128)(2,1)S(1)}, u32[]{:S(2)}, u32[]{:S(2)}) async-start(bf16[16,128,80]{2,0,1:T(8,128)(2,1)} %copy.8), calls=%async_computation | async-start | bytes 1048576 | tf_op jit(solution)/shard_map/all_to_all | solution.py:46
  30.6 0.6 reshape.25
  31.3 0.1 copy.10
  31.4 1.1 copy.11
  32.5 30.4 %all-to-all-done = bf16[16,128,80]{2,0,1:T(8,128)(2,1)S(1)} async-done(((bf16[16,128,80]{2,0,1:T(8,128)(2,1)}), bf16[16,128,80]{2,0,1:T(8,128)(2,1)S(1)}, u32[]{:S(2)}, u32[]{:S(2)}) %all-to-all-start) | async-done | bytes 327712 | tf_op jit(solution)/shard_map/all_to_all | solution.py:46
  62.9 7.6 %all-to-all-start.2 = ((bf16[16,128,80]{2,0,1:T(8,128)(2,1)}), bf16[16,128,80]{2,0,1:T(8,128)(2,1)S(1)}, u32[]{:S(2)}, u32[]{:S(2)}) async-start(bf16[16,128,80]{2,0,1:T(8,128)(2,1)} %copy.11), calls=%async_computation.2 | async-start | bytes 1048576 | tf_op jit(solution)/shard_map/all_to_all | solution.py:47
  70.6 0.2 copy.9
  70.8 32.1 %all-to-all-done.2 = bf16[16,128,80]{2,0,1:T(8,128)(2,1)S(1)} async-done(((bf16[16,128,80]{2,0,1:T(8,128)(2,1)}), bf16[16,128,80]{2,0,1:T(8,128)(2,1)S(1)}, u32[]{:S(2)}, u32[]{:S(2)}) %all-to-all-start.2) | async-done | bytes 327712 | tf_op jit(solution)/shard_map/all_to_all | solution.py:47
  102.8 3.0 stack.5
  105.8 5.3 %all-to-all-start.1 = ((bf16[16,2048,80]{1,2,0:T(8,128)(2,1)}), bf16[16,2048,80]{1,2,0:T(8,128)(2,1)}, u32[]{:S(2)}, u32[]{:S(2)}) async-start(bf16[16,2048,80]{1,2,0:T(8,128)(2,1)} %stack.5), calls=%async_computation.1 | async-start | bytes 10485760 | tf_op jit(solution)/shard_map/all_to_all | solution.py:11
  111.2 0.0 all-gather.2.cloned.1.call-start
  111.2 0.9 copy.12
  112.1 0.0 all-gather.2.cloned.1.call-update
  112.2 0.0 all-reduce.2.cloned.1.call-start
  112.2 35.4 %all-gather.2.cloned.1.call-done = bf16[2048,640]{0,1:T(8,128)(2,1)} async-done(((bf16[2048,80]{0,1:T(8,128)(2,1)}), bf16[2048,640]{0,1:T(8,128)(2,1)}) %all-gather.2.cloned.1.call-update) | async-done | bytes 2621456 | tf_op jit(solution)/shard_map/all_gather | solution.py:49
  147.6 190.2 %all-to-all-done.1 = bf16[16,2048,80]{1,2,0:T(8,128)(2,1)} async-done(((bf16[16,2048,80]{1,2,0:T(8,128)(2,1)}), bf16[16,2048,80]{1,2,0:T(8,128)(2,1)}, u32[]{:S(2)}, u32[]{:S(2)}) %all-to-all-start.1) | async-done | bytes 5242912 | tf_op jit(solution)/shard_map/all_to_all | solution.py:11
  337.9 9.3 %fusion = f32[1280,640]{1,0:T(8,128)} fusion(bf16[2048,1280]{0,1:T(8,128)(2,1)} %bitcast.5, bf16[2048,640]{0,1:T(8,128)(2,1)} %all-gather.2.cloned.1.call-done), kind=kOutput, calls=%fused_computation.6 | convolution fusion | flops 3355443200 | bytes 11141120 | tf_op jit(solution)/shard_map/dot_general | solution.py:50
  347.2 92.6 %all-reduce.2.cloned.1.call-done = f32[1280,640]{1,0:T(8,128)} async-done(((f32[1280,640]{1,0:T(8,128)}), f32[1280,640]{1,0:T(8,128)}) %all-reduce.2.cloned.1.call-update) | async-done | bytes 3276816 | tf_op jit(solution)/shard_map/psum | solution.py:59
  439.8 3.5 select_convert_fusion
  (3 shorter events, 0.0 us)
Async XLA Ops:
  10.2 52.7 %all-to-all-start = ((bf16[16,128,80]{2,0,1:T(8,128)(2,1)}), bf16[16,128,80]{2,0,1:T(8,128)(2,1)S(1)}, u32[]{:S(2)}, u32[]{:S(2)}) async-start(bf16[16,128,80]{2,0,1:T(8,128)(2,1)} %copy.8), calls=%async_computation | async-start | bytes 1048576 | tf_op jit(solution)/shard_map/all_to_all | solution.py:46
  62.9 39.9 %all-to-all-start.2 = ((bf16[16,128,80]{2,0,1:T(8,128)(2,1)}), bf16[16,128,80]{2,0,1:T(8,128)(2,1)S(1)}, u32[]{:S(2)}, u32[]{:S(2)}) async-start(bf16[16,128,80]{2,0,1:T(8,128)(2,1)} %copy.11), calls=%async_computation.2 | async-start | bytes 1048576 | tf_op jit(solution)/shard_map/all_to_all | solution.py:47
  105.8 232.0 %all-to-all-start.1 = ((bf16[16,2048,80]{1,2,0:T(8,128)(2,1)}), bf16[16,2048,80]{1,2,0:T(8,128)(2,1)}, u32[]{:S(2)}, u32[]{:S(2)}) async-start(bf16[16,2048,80]{1,2,0:T(8,128)(2,1)} %stack.5), calls=%async_computation.1 | async-start | bytes 10485760 | tf_op jit(solution)/shard_map/all_to_all | solution.py:11
  111.2 36.5 %all-gather.2.cloned.1.call-start = ((), (), s32[]{:S(2)}) async-start(), calls=%async_computation.3 | async-start | bytes 2949120 | tf_op jit(solution)/shard_map/all_gather | solution.py:49
  112.2 327.6 %all-reduce.2.cloned.1.call-start = ((), (), s32[]{:S(2)}) async-start(), calls=%async_computation.4 | async-start | bytes 6553600 | tf_op jit(solution)/shard_map/psum | solution.py:59
Sparse Core Ops, SparseCore 0:
  114.1 33.4 all-gather.1
  347.3 92.4 all-reduce.1
